TPU v7x, 256 devices: a whole 4x4x8 slice. The times are simulated.
256 devices in a mesh: out: 128 (over z, y, x), con: 2 (over core).
Axes of the slice: x: 4, y: 4, z: 8, core: 2. Of those that a mesh axis runs over, the one named last changes fastest.
Arguments:
- amplitudes: bfloat16 [512, 9216], P(('out', 'con')), may hold values from -6 to 6
- integrals: bfloat16 [131072, 9216], P('out', 'con'), may hold values from -0.078125 to 0.078125
- block_sizes: int32 [8], replicated, may hold values from 64 to 192, as said below
Outputs:
- ladder: bfloat16 [512, 131072], P('con', 'out')
Inputs may be any that keep to these rules, and one draw needn't show every extreme that they name: `block_sizes`: each entry lies between 64 and 192; the entries sum to 1024; one entry equals 192 and one equals 64.
All inputs are finite; a program needn't handle non-finite values.
Results may differ from a plain program's by a relative error of at most 0.001.
Values may be sent and summed in bfloat16 or wider, within the bound.
A program may use at most 64 MiB of HBM per device.

v0:
```python
import jax
import jax.numpy as jnp
from jax import lax
from jax.sharding import PartitionSpec as P

DMAX = 192


def mask_slots(amplitudes, block_sizes):
    row_count = amplitudes.shape[0]
    nirrep = block_sizes.shape[0]
    blocked = amplitudes.reshape(row_count, nirrep, -1, DMAX)
    valid_cols = jnp.arange(DMAX, dtype=jnp.int32)[None, :] < block_sizes[:, None]
    masked = jnp.where(valid_cols[None, :, None, :], blocked, jnp.zeros((), amplitudes.dtype))
    return masked.reshape(row_count, -1)


def contract(amp_rows, integrals):
    return lax.dot_general(
        amp_rows, integrals, (((1,), (1,)), ((), ())), preferred_element_type=jnp.float32
    )


def on_device(amplitudes, integrals, block_sizes):
    masked = mask_slots(amplitudes, block_sizes)
    con = lax.axis_index("con")
    con_count = lax.axis_size("con")
    half = integrals.shape[1]
    chip_rows = lax.all_gather(masked, "con", axis=0, tiled=True)
    own_cols = lax.dynamic_slice_in_dim(chip_rows, con * half, half, axis=1)
    all_rows = lax.all_gather(own_cols, "out", axis=0, tiled=True)
    out_rows = all_rows.shape[0] // con_count
    other = 1 - con
    other_part = contract(
        lax.dynamic_slice_in_dim(all_rows, other * out_rows, out_rows, axis=0), integrals
    )
    received = lax.ppermute(other_part, "con", perm=[(0, 1), (1, 0)])
    own_part = contract(
        lax.dynamic_slice_in_dim(all_rows, con * out_rows, out_rows, axis=0), integrals
    )
    own_part = lax.optimization_barrier(own_part)
    return (own_part + received).astype(jnp.bfloat16)


def solution(mesh):
    in_specs = (P(("out", "con"), None), P("out", "con"), P())
    out_specs = P("con", "out")
    return jax.shard_map(
        on_device, mesh=mesh, in_specs=in_specs, out_specs=out_specs, check_vma=False
    )
```

profile of v0, /device:TPU:1, one launch (start us, length us, event | category | flops | bytes accessed | tf_op | source)
XLA Modules:
  0.0 160.5 jit_solution(4676826917405376229)
XLA Ops:
  6.5 0.0 all-gather.4.cloned.1.call-start
  6.5 0.7 iota_compare_fusion
  7.3 0.1 broadcast_in_dim.20
  7.4 0.8 fusion.4
  8.2 4.8 %all-gather = bf16[2,2,9216]{2,1,0:T(2,128)(2,1)S(1)} all-gather(bf16[1,2,9216]{2,1,0:T(2,128)(2,1)S(1)} %fusion.4), channel_id=1, replica_groups=mesh['out'=128,'con'=2] {'con'}, dimensions={0}, use_global_device_ids=true | all-gather | bytes 110592 | tf_op jit(solution)/shard_map/all_gather | solution.py:29
  13.0 0.6 dynamic-slice_bitcast_fusion
  13.7 0.0 all-gather.4.cloned.1.call-update
  13.7 115.3 %all-gather.4.cloned.1.call-done = bf16[128,4,4608]{2,1,0:T(4,128)(2,1)} async-done(((bf16[1,4,4608]{2,1,0:T(4,128)(2,1)}), bf16[128,4,4608]{2,1,0:T(4,128)(2,1)}) %all-gather.4.cloned.1.call-update) | async-done | bytes 4718608 | tf_op jit(solution)/shard_map/all_gather | solution.py:31
  129.0 7.2 %reshape.24 = bf16[512,4608]{1,0:T(8,128)(2,1)} reshape(bf16[128,4,4608]{2,1,0:T(4,128)(2,1)} %all-gather.4.cloned.1.call-done) | data formatting | bytes 9437184
  136.2 6.0 %fusion = f32[256,1024]{1,0:T(8,128)S(1)} fusion(bf16[1024,4608]{1,0:T(8,128)(2,1)} %param.4, bf16[512,4608]{1,0:T(8,128)(2,1)} %reshape.24, s32[]{:T(128)S(6)} %select_n.17), kind=kOutput, calls=%fused_computation | convolution fusion | flops 2415919104 | bytes 12845060 | tf_op jit(solution)/shard_map/dot_general | solution.py:19
  142.2 4.5 %collective-permute-start = (f32[256,1024]{1,0:T(8,128)S(1)}, f32[256,1024]{1,0:T(8,128)S(1)}, u32[]{:S(2)}, u32[]{:S(2)}) collective-permute-start(f32[256,1024]{1,0:T(8,128)S(1)} %fusion), channel_id=1, source_target_pairs={{0,1},{1,0},{2,3},{3,2},{4,5},{5,4},{6,7},{7,6},{8,9},{9,8},{10,11... | collective-permute-start | bytes 3145736 | tf_op jit(solution)/shard_map/ppermute | solution.py:37
  146.7 6.0 %fusion.2 = f32[256,1024]{1,0:T(8,128)S(1)} fusion(bf16[1024,4608]{1,0:T(8,128)(2,1)} %param.4, bf16[512,4608]{1,0:T(8,128)(2,1)} %reshape.24, s32[]{:T(128)S(6)} %select_n.16), kind=kOutput, calls=%fused_computation.2 | convolution fusion | flops 2415919104 | bytes 12845060 | tf_op jit(solution)/shard_map/dot_general | solution.py:19
  152.7 0.0 collective-permute-done
  152.7 1.0 add_convert_fusion
  (2 shorter events, 0.0 us)
Async XLA Ops:
  6.5 122.5 %all-gather.4.cloned.1.call-start = ((), (), s32[]{:S(2)}) async-start(), calls=%async_computation | async-start | bytes 4755456 | tf_op jit(solution)/shard_map/all_gather | solution.py:31
  142.2 10.5 %collective-permute-start = (f32[256,1024]{1,0:T(8,128)S(1)}, f32[256,1024]{1,0:T(8,128)S(1)}, u32[]{:S(2)}, u32[]{:S(2)}) collective-permute-start(f32[256,1024]{1,0:T(8,128)S(1)} %fusion), channel_id=1, source_target_pairs={{0,1},{1,0},{2,3},{3,2},{4,5},{5,4},{6,7},{7,6},{8,9},{9,8},{10,11... | collective-permute-start | bytes 3145736 | tf_op jit(solution)/shard_map/ppermute | solution.py:37
Sparse Core Ops, SparseCore 0:
  13.8 115.1 all-gather.3
where the time goes:
time: 161 us; the launch traced here: 160 us
  waiting for transfers between devices  115 us (71%)
  between operations  13.4 us (8%)
  matrix products  11.9 us (7%)
  local copies, waits for them, and re-layouts  8.04 us (5%)
  blocking collectives  4.75 us (3%)
  starting transfers between devices  4.49 us (3%)
  other arithmetic  2.51 us (2%)
    all_gather x1, waiting for transfers between devices, on_device(): all_rows = lax.all_gather(own_cols, 'out', axis=0, tiled=True)  115 us
    dot_general x2, matrix products, contract(): lax.dot_general(amp_rows, integrals, (((1,), (1,)), ((), ())), preferred_...  11.9 us
    unnamed x3, local copies, waits for them, and re-layouts  7.92 us
    all_gather x1, blocking collectives, on_device(): chip_rows = lax.all_gather(masked, 'con', axis=0, tiled=True)  4.75 us
    ppermute x1, starting transfers between devices, on_device(): received = lax.ppermute(other_part, 'con', perm=[(0, 1), (1, 0)])  4.49 us
  transfers between devices with their start and end apart: 2, of which 1 were waited for; matrix products, arithmetic and copies ran while one was open for 4% of the time, Pallas kernels for 0%

commit v1 on v0

--- a/solution.py
+++ b/solution.py
@@ -26,7 +26,9 @@
     con = lax.axis_index("con")
     con_count = lax.axis_size("con")
     half = integrals.shape[1]
-    chip_rows = lax.all_gather(masked, "con", axis=0, tiled=True)
+    chip_rows = jnp.concatenate(
+        lax.all_to_all(jnp.stack([masked] * lax.axis_size("con")), "con", 0, 0), axis=0
+    )
     own_cols = lax.dynamic_slice_in_dim(chip_rows, con * half, half, axis=1)
     all_rows = lax.all_gather(own_cols, "out", axis=0, tiled=True)
     out_rows = all_rows.shape[0] // con_count

time: 161 us -> 167 us (1.037)
  starting transfers between devices: 4.49 us -> 11 us
  blocking collectives: 4.75 us -> 0 us
  waiting for transfers between devices: 115 us -> 119 us
    all_to_all x0 -> x1, starting transfers between devices: none -> 6.54 us  [on_device(): lax.all_to_all(jnp.stack([masked] * lax.axis_size('con')), 'con', 0, 0)]
    all_gather x1 -> x0, blocking collectives: 4.75 us -> none  [on_device(): chip_rows = lax.all_gather(masked, 'con', axis=0, tiled=True)]
    all_gather x1, waiting for transfers between devices: 115 us -> 118 us  [on_device(): all_rows = lax.all_gather(own_cols, 'out', axis=0, tiled=True)]
    unnamed x3 -> x2, local copies, waits for them, and re-layouts: 7.92 us -> 7.87 us
  transfers between devices with their start and end apart: 2 -> 3, of which waited for: 1 -> 2; matrix products, arithmetic and copies ran while one was open for 4% -> 4% of each run, Pallas kernels for 0% -> 0%
where the time goes in v1:
time: 167 us; the launch traced here: 166 us
  waiting for transfers between devices  119 us (71%)
  between operations  13.4 us (8%)
  matrix products  11.9 us (7%)
  starting transfers between devices  11 us (7%)
  local copies, waits for them, and re-layouts  8.03 us (5%)
  other arithmetic  3.2 us (2%)
    all_gather x1, waiting for transfers between devices, on_device(): all_rows = lax.all_gather(own_cols, 'out', axis=0, tiled=True)  118 us
    dot_general x2, matrix products, contract(): lax.dot_general(amp_rows, integrals, (((1,), (1,)), ((), ())), preferred_...  11.9 us
    unnamed x2, local copies, waits for them, and re-layouts  7.87 us
    all_to_all x1, starting transfers between devices, on_device(): lax.all_to_all(jnp.stack([masked] * lax.axis_size('con')), 'con', 0, 0)  6.54 us
    ppermute x1, starting transfers between devices, on_device(): received = lax.ppermute(other_part, 'con', perm=[(0, 1), (1, 0)])  4.5 us
  transfers between devices with their start and end apart: 3, of which 2 were waited for; matrix products, arithmetic and copies ran while one was open for 4% of the time, Pallas kernels for 0%

profile of v1, /device:TPU:1, one launch (start us, length us, event | category | flops | bytes accessed | tf_op | source)
XLA Modules:
  0.0 166.3 jit_solution(18214157720322139895)
XLA Ops:
  6.5 0.7 iota_compare_fusion
  7.3 0.1 broadcast_in_dim.20
  7.4 0.8 fusion.4
  8.2 0.7 pad_maximum_fusion
  8.9 6.5 %all-to-all-start = ((bf16[2,2,9216]{2,1,0:T(2,128)(2,1)}), bf16[2,2,9216]{2,1,0:T(2,128)(2,1)S(1)}, u32[]{:S(2)}, u32[]{:S(2)}) async-start(bf16[2,2,9216]{2,1,0:T(2,128)(2,1)} %pad_maximum_fusion), calls=%async_computation | async-start | bytes 147456 | tf_op jit(solution)/shard_map/all_to_all | solution.py:30
  15.5 0.0 all-gather.3.cloned.1.call-start
  15.5 1.1 all-to-all-done
  16.6 0.6 dynamic-slice_bitcast_fusion
  17.2 0.0 all-gather.3.cloned.1.call-update
  17.2 117.6 %all-gather.3.cloned.1.call-done = bf16[128,4,4608]{2,1,0:T(4,128)(2,1)} async-done(((bf16[1,4,4608]{2,1,0:T(4,128)(2,1)}), bf16[128,4,4608]{2,1,0:T(4,128)(2,1)}) %all-gather.3.cloned.1.call-update) | async-done | bytes 4718608 | tf_op jit(solution)/shard_map/all_gather | solution.py:33
  134.8 7.2 %reshape.27 = bf16[512,4608]{1,0:T(8,128)(2,1)} reshape(bf16[128,4,4608]{2,1,0:T(4,128)(2,1)} %all-gather.3.cloned.1.call-done) | data formatting | bytes 9437184
  142.1 6.0 %fusion = f32[256,1024]{1,0:T(8,128)S(1)} fusion(bf16[1024,4608]{1,0:T(8,128)(2,1)} %param.4, bf16[512,4608]{1,0:T(8,128)(2,1)} %reshape.27, s32[]{:T(128)S(6)} %select_n.21), kind=kOutput, calls=%fused_computation | convolution fusion | flops 2415919104 | bytes 12845060 | tf_op jit(solution)/shard_map/dot_general | solution.py:19
  148.0 4.5 %collective-permute-start = (f32[256,1024]{1,0:T(8,128)S(1)}, f32[256,1024]{1,0:T(8,128)S(1)}, u32[]{:S(2)}, u32[]{:S(2)}) collective-permute-start(f32[256,1024]{1,0:T(8,128)S(1)} %fusion), channel_id=1, source_target_pairs={{0,1},{1,0},{2,3},{3,2},{4,5},{5,4},{6,7},{7,6},{8,9},{9,8},{10,11... | collective-permute-start | bytes 3145736 | tf_op jit(solution)/shard_map/ppermute | solution.py:39
  152.5 6.0 %fusion.2 = f32[256,1024]{1,0:T(8,128)S(1)} fusion(bf16[1024,4608]{1,0:T(8,128)(2,1)} %param.4, bf16[512,4608]{1,0:T(8,128)(2,1)} %reshape.27, s32[]{:T(128)S(6)} %select_n.20), kind=kOutput, calls=%fused_computation.2 | convolution fusion | flops 2415919104 | bytes 12845060 | tf_op jit(solution)/shard_map/dot_general | solution.py:19
  158.5 0.0 collective-permute-done
  158.5 1.0 add_convert_fusion
  (2 shorter events, 0.0 us)
Async XLA Ops:
  8.9 7.6 %all-to-all-start = ((bf16[2,2,9216]{2,1,0:T(2,128)(2,1)}), bf16[2,2,9216]{2,1,0:T(2,128)(2,1)S(1)}, u32[]{:S(2)}, u32[]{:S(2)}) async-start(bf16[2,2,9216]{2,1,0:T(2,128)(2,1)} %pad_maximum_fusion), calls=%async_computation | async-start | bytes 147456 | tf_op jit(solution)/shard_map/all_to_all | solution.py:30
  15.5 119.4 %all-gather.3.cloned.1.call-start = ((), (), s32[]{:S(2)}) async-start(), calls=%async_computation.1 | async-start | bytes 4755456 | tf_op jit(solution)/shard_map/all_gather | solution.py:33
  148.0 10.5 %collective-permute-start = (f32[256,1024]{1,0:T(8,128)S(1)}, f32[256,1024]{1,0:T(8,128)S(1)}, u32[]{:S(2)}, u32[]{:S(2)}) collective-permute-start(f32[256,1024]{1,0:T(8,128)S(1)} %fusion), channel_id=1, source_target_pairs={{0,1},{1,0},{2,3},{3,2},{4,5},{5,4},{6,7},{7,6},{8,9},{9,8},{10,11... | collective-permute-start | bytes 3145736 | tf_op jit(solution)/shard_map/ppermute | solution.py:39
Sparse Core Ops, SparseCore 0:
  20.1 114.6 all-gather.2
